TPU v7x, 256 devices: a whole 4x4x8 slice. The times are simulated.
256 devices in a mesh: blk: 32 (over y, z), rep: 8 (over x, core).
Axes of the slice: x: 4, y: 4, z: 8, core: 2. Of those that a mesh axis runs over, the one named last changes fastest.
Arguments:
- hidden_in: bfloat16 [8, 512, 2560], P('rep', 'blk'), may hold values from -6 to 6
- w_z: bfloat16 [2560, 4096], P(None, 'blk'), may hold values from -0.125 to 0.125
- w_x: bfloat16 [2560, 4096], P(None, 'blk'), may hold values from -0.125 to 0.125
- w_bc: bfloat16 [2560, 256], replicated, may hold values from -0.125 to 0.125
- w_dt: bfloat16 [2560, 64], P(None, 'blk'), may hold values from -0.125 to 0.125
- conv_x: float32 [4, 4096], P(None, 'blk'), may hold values from -3 to 3
- conv_bc: float32 [4, 256], replicated, may hold values from -3 to 3
- dt_bias: float32 [4, 64], P(None, 'blk'), may hold values from -3 to -0.5
- a_log: float32 [64], P('blk'), may hold values from -2.5 to 0.5
- d_skip: float32 [64], P('blk'), may hold values from 0.5 to 1.5
- norm_gain: float32 [4096], P('blk'), may hold values from 0.5 to 1.5
- w_out: bfloat16 [4096, 2560], P('blk'), may hold values from -0.09375 to 0.09375
- edge_x: bfloat16 [256, 3, 4096], P('rep', None, 'blk'), may hold values from -6 to 6
- edge_bc: bfloat16 [256, 3, 256], P('rep'), may hold values from -6 to 6
- pool: float32 [384, 64, 64, 128], P('rep', 'blk'), may hold values from -0.6 to 0.6
- tenant_sizes: int32 [4], replicated, may hold values from 1 to 128, 256 in all
- owner: int32 [256, 1], P('rep'), may hold values from 0 to 7; in each aligned block of 32 rows (0 to 31, 32 to 63, ...) at most 6 rows name the same one
- accepted: int32 [256], P('rep'), may hold values from 1 to 16
- prompt_len: int32 [256], P('rep'), may hold values from 1 to 11
Outputs:
- hidden_out: bfloat16 [8, 512, 2560], P('rep', 'blk')
- new_pool: float32 [384, 64, 64, 128], P('rep', 'blk')
Inputs may be any that keep to these rules, and one draw needn't show every extreme that they name: Among the requests of one group (aligned blocks of 32 requests) each owner is named at most 6 times, a bound that some block reaches. `tenant_sizes`: the sizes sum to 256.
All inputs are finite; a program needn't handle non-finite values.
Results may differ from a plain program's by a relative error of at most 0.025.
Values may be sent and summed in bfloat16 or wider, within the bound.
A program may use at most 64 MiB of HBM per device.

v0:
```python
import jax
import jax.numpy as jnp
from jax import lax
from jax.sharding import PartitionSpec as P


def convolve(edge_cells, fresh_cells, kernel, edge_mask):
    sequence = jnp.concatenate(
        [edge_cells * edge_mask[:, :, None].astype(edge_cells.dtype), fresh_cells], 1
    ).astype(jnp.float32)
    steps_count = fresh_cells.shape[1]
    summed = kernel[0] * sequence[:, 0:steps_count]
    for offset in range(1, kernel.shape[0]):
        summed = summed + kernel[offset] * sequence[:, offset : offset + steps_count]
    return jax.nn.silu(summed).astype(jnp.bfloat16)


def shards(
    hidden_in,
    w_z,
    w_x,
    w_bc,
    w_dt,
    conv_x,
    conv_bc,
    dt_bias,
    a_log,
    d_skip,
    norm_gain,
    w_out,
    edge_x,
    edge_bc,
    pool,
    tenant_sizes,
    owner,
    accepted,
    prompt_len,
):
    highest = lax.Precision.HIGHEST
    rows_in = hidden_in[0]
    local_rows = rows_in.shape[0]
    n_req = edge_x.shape[0]
    drafts = local_rows * lax.axis_size("blk") // n_req
    state_dim = w_bc.shape[1] // 2
    heads_here = w_dt.shape[1]
    inner_here = w_z.shape[1]
    head_dim = inner_here // heads_here
    slots_here = pool.shape[0]
    cap_group = slots_here // lax.axis_size("rep")
    weights_in = (w_z, w_x, w_dt, w_bc)
    block_rows = lax.all_gather(rows_in, "blk", axis=0, tiled=True)
    projected = jnp.concatenate(
        [
            jnp.dot(block_rows, weight_cols, preferred_element_type=jnp.float32)
            for weight_cols in weights_in
        ],
        1,
    ).astype(jnp.bfloat16)
    z_all = projected[:, :inner_here]
    u_all = projected[:, inner_here : 2 * inner_here]
    dt_raw = projected[:, 2 * inner_here : 2 * inner_here + heads_here]
    bc_all = projected[:, 2 * inner_here + heads_here :]
    edge_len = edge_x.shape[1]
    edge_mask = prompt_len[:, None] >= (edge_len - jnp.arange(edge_len, dtype=jnp.int32))[None, :]
    x_conv = convolve(edge_x, u_all.reshape(n_req, drafts, inner_here), conv_x, edge_mask)
    bc_conv = convolve(edge_bc, bc_all.reshape(n_req, drafts, 2 * state_dim), conv_bc, edge_mask)
    b_half = bc_conv[:, :, :state_dim]
    c_half = bc_conv[:, :, state_dim:]
    b_float = b_half.astype(jnp.float32)
    c_float = c_half.astype(jnp.float32)
    x_heads = x_conv.reshape(n_req, drafts, heads_here, head_dim).astype(jnp.float32)
    req_index = lax.axis_index("rep") * n_req + jnp.arange(n_req, dtype=jnp.int32)
    tenant_ends = jnp.cumsum(tenant_sizes)
    tenant_id = jnp.sum((req_index[:, None] >= tenant_ends[None, :-1]).astype(jnp.int32), axis=1)
    tenant_pick = (
        tenant_id[:, None] == jnp.arange(tenant_sizes.shape[0], dtype=jnp.int32)[None, :]
    ).astype(jnp.float32)
    bias_req = jnp.dot(tenant_pick, dt_bias, precision=highest)
    step_size = jax.nn.softplus(
        dt_raw.reshape(n_req, drafts, heads_here).astype(jnp.float32) + bias_req[:, None, :]
    )
    log_decay = jnp.cumsum(step_size * (-jnp.exp(a_log))[None, None, :], axis=1)
    draft_index = jnp.arange(drafts, dtype=jnp.int32)
    causal = draft_index[:, None] >= draft_index[None, :]
    scores = jnp.einsum("rtn,rsn->rts", c_float, b_float, precision=highest)
    log_gap = log_decay[:, :, None, :] - log_decay[:, None, :, :]
    weight = (
        jnp.where(causal[None, :, :, None], jnp.exp(jnp.minimum(log_gap, 0.0)), 0.0)
        * step_size[:, None, :, :]
        * scores[:, :, :, None]
    )
    y_local = (
        jnp.einsum("rtsh,rshp->rthp", weight, x_heads, precision=highest)
        + d_skip[None, None, :, None] * x_heads
    )
    pick_last = (draft_index[None, :] == accepted[:, None] - 1).astype(jnp.float32)
    log_accept = jnp.sum(pick_last[:, :, None] * log_decay, axis=1)
    keep_draft = draft_index[None, :] < accepted[:, None]
    coef = (
        jnp.where(
            keep_draft[:, :, None],
            jnp.exp(jnp.minimum(log_accept[:, None, :] - log_decay, 0.0)),
            0.0,
        )
        * step_size
    )
    carry_decay = jnp.exp(log_accept)
    decay_now = jnp.exp(log_decay)
    owner_of = owner[:, 0]
    local_index = jnp.arange(n_req, dtype=jnp.int32)
    earlier = (owner_of[None, :] == owner_of[:, None]) & (
        local_index[None, :] < local_index[:, None]
    )
    rank_within = jnp.sum(earlier.astype(jnp.int32), axis=1)
    slot_index = owner_of * cap_group + rank_within
    fetched = lax.all_to_all(
        pool.astype(jnp.bfloat16), "rep", split_axis=0, concat_axis=0, tiled=True
    ).astype(pool.dtype)
    start_state = jnp.take(fetched, slot_index, axis=0)
    y_prior = decay_now[:, :, :, None] * jnp.einsum(
        "rhpn,rtn->rthp", start_state, c_float, precision=highest
    )
    accepted_state = carry_decay[:, :, None, None] * start_state + jnp.einsum(
        "rsh,rshp,rsn->rhpn", coef, x_heads, b_float, precision=highest
    )
    buffer = jnp.zeros(pool.shape, jnp.float32).at[slot_index].set(accepted_state)
    new_pool = lax.all_to_all(
        buffer.astype(jnp.bfloat16), "rep", split_axis=0, concat_axis=0, tiled=True
    ).astype(buffer.dtype)
    y_total = (y_local + y_prior).reshape(n_req * drafts, inner_here)
    gated = y_total * jax.nn.silu(z_all.astype(jnp.float32))
    sq_total = lax.psum(jnp.sum(gated * gated, axis=1), "blk")
    inner_all = inner_here * lax.axis_size("blk")
    normed = (gated * lax.rsqrt(sq_total / inner_all + 1e-05)[:, None] * norm_gain[None, :]).astype(
        jnp.bfloat16
    )
    block_rows = normed
    mixed = lax.psum_scatter(
        jnp.dot(block_rows, w_out, preferred_element_type=jnp.float32).astype(jnp.bfloat16),
        "blk",
        scatter_dimension=0,
        tiled=True,
    )
    return (mixed[None], new_pool)


def solution(mesh):
    placed = (
        P("rep", "blk", None),
        P(None, "blk"),
        P(None, "blk"),
        P(),
        P(None, "blk"),
        P(None, "blk"),
        P(),
        P(None, "blk"),
        P("blk"),
        P("blk"),
        P("blk"),
        P("blk", None),
        P("rep", None, "blk"),
        P("rep", None, None),
        P("rep", "blk", None, None),
        P(),
        P("rep", None),
        P("rep"),
        P("rep"),
    )
    return jax.shard_map(
        shards,
        mesh=mesh,
        in_specs=placed,
        out_specs=(P("rep", "blk", None), P("rep", "blk", None, None)),
        check_vma=False,
    )
```

profile of v0, /device:TPU:2, one launch (start us, length us, event | category | flops | bytes accessed | tf_op | source)
XLA Modules:
  0.0 418.3 jit_solution(11525417549869949106)
XLA Ops:
  7.2 0.7 all-gather.3.cloned.1.call-update
  7.9 3.4 convert_element_type.82
  11.4 5.9 %all-to-all-start = ((bf16[48,2,64,128]{3,2,1,0:T(8,128)(2,1)}), bf16[48,2,64,128]{3,2,1,0:T(8,128)(2,1)S(1)}, u32[]{:S(2)}, u32[]{:S(2)}) async-start(bf16[48,2,64,128]{3,2,1,0:T(8,128)(2,1)} %convert_element_type.82), calls=%async_computation | async-start | bytes 3145728 | tf_op jit(solution)/shard_map/all_to_all | solution.py:116
  17.7 0.5 and_bitcast_fusion
  18.4 0.5 copy-done.10
  19.0 0.6 iota_compare_fusion.5
  19.6 0.6 copy.75
  20.3 0.2 fusion.70
  20.4 0.6 slice_bitcast_fusion.4
  21.1 0.6 fusion.75
  21.7 0.6 fusion.72
  22.3 0.7 copy_multiply_fusion
  23.0 14.5 %all-to-all-done = bf16[48,2,64,128]{3,2,1,0:T(8,128)(2,1)S(1)} async-done(((bf16[48,2,64,128]{3,2,1,0:T(8,128)(2,1)}), bf16[48,2,64,128]{3,2,1,0:T(8,128)(2,1)S(1)}, u32[]{:S(2)}, u32[]{:S(2)}) %all-to-all-start) | async-done | bytes 1572896 | tf_op jit(solution)/shard_map/all_to_all | solution.py:116
  37.5 2.1 convert_element_type.83
  39.5 2.6 gather_fusion
  42.1 50.4 %all-gather.3.cloned.1.call-done = bf16[1,512,2560]{2,1,0:T(8,128)(2,1)} async-done(((bf16[1,16,2560]{2,1,0:T(8,128)(2,1)}), bf16[1,512,2560]{2,1,0:T(8,128)(2,1)}) %all-gather.3.cloned.1.call-update) | async-done | bytes 2621456 | tf_op jit(solution)/shard_map/all_gather | solution.py:51
  92.5 2.5 fusion.32
  95.2 0.7 broadcast_multiply_fusion.1
  95.9 0.7 copy.80
  96.6 2.7 fusion.20
  99.4 0.2 multiply_convert_fusion.2
  99.6 0.9 reshape.167
  100.5 1.6 copy.77
  102.0 1.7 fusion.76
  103.7 1.2 copy.78
  104.9 1.7 multiply_reduce_fusion
  106.7 1.2 copy.85
  107.9 2.6 fusion.17
  110.7 0.3 multiply_convert_fusion
  111.1 0.2 fusion.65
  111.3 0.2 copy-done.3
  111.5 0.6 fusion.16
  112.1 2.6 fusion.13
  114.8 1.1 copy.86
  115.8 2.0 reshape.170
  117.9 1.8 copy.87
  119.7 3.7 multiply_reduce_fusion.1
  123.4 72.2 %psum.7 = f32[512]{0:T(512)S(1)} all-reduce(f32[512]{0:T(512)S(1)} %get-tuple-element.16), channel_id=1, replica_groups=mesh['blk'=32,'rep'=8] {'blk'}, use_global_device_ids=true, to_apply=%region_5.6 | all-reduce | flops 512 | bytes 4096 | tf_op jit(solution)/shard_map/psum | solution.py:132
  195.6 3.6 convolution_convert_fusion
  199.2 0.6 copy-done.26
  199.9 1.1 copy.89
  201.2 4.6 %multiply_add_fusion = f32[32,2,64,128]{3,2,1,0:T(8,128)} fusion(f32[32,2,64,128]{3,2,1,0:T(8,128)S(1)} %gather_fusion, f32[32,2]{1,0:T(8,128)S(1)} %exp.50, pred[32]{0:T(512)(128)(4,1)S(1)} %copy-done.12, f32[32,16,2]{1,2,0:T(2,128)S(1)} %copy.90, bf16[32,16,2,64]{3,2,1,0:T(2,128)(2,1)} %reshape.167, bf16[32,16,256]{2,1,0:T(8,128)(2,1)} %copy-done.2), kind=kOutput, calls=%fused_computation.11 | convolution fusion | flops 102367232 | bytes 4591904 | tf_op jit(solution)/shard_map/rsh,rshp,rsn->rhpn/dot_general | solution.py:123
  205.7 2.1 broadcast_in_dim.31
  207.9 5.3 %scatter_fusion = f32[48,2,64,128]{3,2,1,0:T(8,128)} fusion(f32[48,2,64,128]{3,2,1,0:T(8,128)} %broadcast_in_dim.31, s32[32]{0:T(128)S(1)} %bitcast.79, f32[32,2,64,128]{3,2,1,0:T(8,128)S(1)} %copy-done.1), kind=kCustom, calls=%fused_computation.1 | custom fusion | bytes 6291584 | tf_op jit(solution)/shard_map/scatter | solution.py:126
  213.2 2.3 convert_element_type.88
  215.5 24.9 %all_to_all.10 = bf16[48,2,64,128]{3,2,1,0:T(8,128)(2,1)S(1)} all-to-all(bf16[48,2,64,128]{3,2,1,0:T(8,128)(2,1)S(1)} %convert_element_type.88), channel_id=1, replica_groups=mesh['blk'=32,'rep'=8] {'rep'}, dimensions={0} | all-to-all | bytes 3145728 | tf_op jit(solution)/shard_map/all_to_all | solution.py:127
  240.4 2.0 convert_element_type.89
  242.5 169.0 %reduce-scatter.2.cloned.1.call-done = bf16[16,2560]{1,0:T(8,128)(2,1)} async-done(((bf16[512,2560]{1,0:T(8,128)(2,1)}), bf16[16,2560]{1,0:T(8,128)(2,1)}) %reduce-scatter.2.cloned.1.call-update) | async-done | bytes 81936 | tf_op jit(solution)/shard_map/reduce_scatter | solution.py:138
  (88 shorter events, 1.5 us)
Async XLA Ops:
  7.2 100.7 %copy-start = (bf16[2560,256]{1,0:T(8,128)(2,1)S(1)}, bf16[2560,256]{1,0:T(8,128)(2,1)}, u32[]{:S(2)}) copy-start(bf16[2560,256]{1,0:T(8,128)(2,1)} %param.22) | copy-start | bytes 3932164
  7.2 85.3 %all-gather.3.cloned.1.call-start = ((), (), s32[]{:S(2)}) async-start(), calls=%async_computation.4 | async-start | bytes 2703360 | tf_op jit(solution)/shard_map/all_gather | solution.py:51
  11.3 6.0 %copy-start.30 = (s32[4]{0:T(128)S(1)}, s32[4]{0:T(128)}, u32[]{:S(2)}) copy-start(s32[4]{0:T(128)} %param.34) | copy-start | bytes 52
  11.3 6.2 %copy-start.27 = (s32[32,1]{0,1:T(1,128)S(1)}, s32[32,1]{0,1:T(1,128)}, u32[]{:S(2)}) copy-start(s32[32,1]{0,1:T(1,128)} %param.35) | copy-start | bytes 388
  11.3 7.0 %copy-start.31 = (f32[2]{0:T(128)S(1)}, f32[2]{0:T(128)}, u32[]{:S(2)}) copy-start(f32[2]{0:T(128)} %param.27) | copy-start | bytes 28
  11.3 7.5 %copy-start.28 = (s32[32]{0:T(128)S(1)}, s32[32]{0:T(128)}, u32[]{:S(2)}) copy-start(s32[32]{0:T(128)} %param.37) | copy-start | bytes 388
  11.3 7.5 %copy-start.8 = (bf16[32,3,128]{2,0,1:T(8,128)(2,1)S(1)}, bf16[32,3,128]{2,0,1:T(8,128)(2,1)}, u32[]{:S(2)}) copy-start(bf16[32,3,128]{2,0,1:T(8,128)(2,1)} %param.31) | copy-start | bytes 73732
  11.4 8.9 %copy-start.25 = (s32[32]{0:T(128)S(1)}, s32[32]{0:T(128)}, u32[]{:S(2)}) copy-start(s32[32]{0:T(128)} %param.36) | copy-start | bytes 388
  11.4 8.9 %copy-start.29 = (f32[4,2]{0,1:T(2,128)S(1)}, f32[4,2]{0,1:T(2,128)}, u32[]{:S(2)}) copy-start(f32[4,2]{0,1:T(2,128)} %param.26) | copy-start | bytes 100
  11.4 9.1 %copy-start.22 = (f32[4,128]{1,0:T(4,128)S(1)}, f32[4,128]{1,0:T(4,128)}, u32[]{:S(2)}) copy-start(f32[4,128]{1,0:T(4,128)} %param.24) | copy-start | bytes 6148
  11.4 9.7 %copy-start.17 = (f32[4,256]{1,0:T(4,128)S(1)}, f32[4,256]{1,0:T(4,128)}, u32[]{:S(2)}) copy-start(f32[4,256]{1,0:T(4,128)} %param.25) | copy-start | bytes 12292
  11.4 10.8 %copy-start.6 = (bf16[32,3,256]{2,0,1:T(8,128)(2,1)S(1)}, bf16[32,3,256]{2,0,1:T(8,128)(2,1)}, u32[]{:S(2)}) copy-start(bf16[32,3,256]{2,0,1:T(8,128)(2,1)} %param.32) | copy-start | bytes 147460
  11.4 26.1 %all-to-all-start = ((bf16[48,2,64,128]{3,2,1,0:T(8,128)(2,1)}), bf16[48,2,64,128]{3,2,1,0:T(8,128)(2,1)S(1)}, u32[]{:S(2)}, u32[]{:S(2)}) async-start(bf16[48,2,64,128]{3,2,1,0:T(8,128)(2,1)} %convert_element_type.82), calls=%async_computation | async-start | bytes 3145728 | tf_op jit(solution)/shard_map/all_to_all | solution.py:116
  17.3 394.1 %reduce-scatter.2.cloned.1.call-start = ((), (), s32[]{:S(2)}) async-start(), calls=%async_computation.3 | async-start | bytes 2703360 | tf_op jit(solution)/shard_map/reduce_scatter | solution.py:138
  18.2 0.6 copy-start.10
  39.5 53.0 %copy-start.9 = (bf16[2560,2]{0,1:T(2,128)(2,1)S(1)}, bf16[2560,2]{0,1:T(2,128)(2,1)}, u32[]{:S(2)}) copy-start(bf16[2560,2]{0,1:T(2,128)(2,1)} %param.23) | copy-start | bytes 30724
  96.6 2.8 copy-start.5
  96.6 2.8 copy-start.18
  96.6 2.8 copy-start.19
  96.6 2.8 copy-start.20
  96.6 2.8 copy-start.21
  107.9 2.7 copy-start.4
  107.9 2.8 copy-start.13
  107.9 2.8 copy-start.14
  107.9 2.8 copy-start.15
  107.9 2.8 copy-start.16
  110.5 1.0 copy-start.3
  110.5 0.9 copy-start.7
  110.6 0.9 copy-start.23
  110.6 0.9 copy-start.32
  110.7 1.4 copy-start.12
  111.1 3.7 copy-start.2
  119.7 75.9 %copy-start.24 = (f32[128]{0:T(128)S(1)}, f32[128]{0:T(128)}, u32[]{:S(2)}) copy-start(f32[128]{0:T(128)} %param.29) | copy-start | bytes 1540
  199.2 0.7 copy-start.26
  205.7 2.1 copy-start.1
  205.7 2.1 copy-start.11
Sparse Core Ops, SparseCore 0:
  10.6 81.8 all-gather.2
  199.3 212.0 reduce-scatter.1
where the time goes:
time: 419 us; the launch traced here: 418 us
  waiting for transfers between devices  235 us (56%)
  blocking collectives  97.1 us (23%)
  local copies, waits for them, and re-layouts  25.3 us (6%)
  matrix products  23.3 us (6%)
  other arithmetic  17.6 us (4%)
  between operations  14.4 us (3%)
  starting transfers between devices  5.94 us (1%)
    reduce_scatter x1, waiting for transfers between devices, shards(): lax.psum_scatter(jnp.dot(block_rows, w_out, preferred_element_type=jnp.fl...  169 us
    psum x1, blocking collectives, shards(): sq_total = lax.psum(jnp.sum(gated * gated, axis=1), 'blk')  72.2 us
    all_gather x1, waiting for transfers between devices, shards(): block_rows = lax.all_gather(rows_in, 'blk', axis=0, tiled=True)  50.4 us
    all_to_all x1, blocking collectives, shards(): lax.all_to_all(buffer.astype(jnp.bfloat16), 'rep', split_axis=0, concat_a...  24.9 us
    all_to_all x1, waiting for transfers between devices, shards(): lax.all_to_all(pool.astype(jnp.bfloat16), 'rep', split_axis=0, concat_axi...  14.5 us
    dot_general x4, matrix products, shards(): jnp.dot(block_rows, weight_cols, preferred_element_type=jnp.float32)  11.5 us
  transfers between devices with their start and end apart: 3, of which 3 were waited for; matrix products, arithmetic and copies ran while one was open for 7% of the time, Pallas kernels for 0%

commit v1 on v0

--- a/solution.py
+++ b/solution.py
@@ -1,7 +1,23 @@
+import functools
 import jax
 import jax.numpy as jnp
 from jax import lax
 from jax.sharding import PartitionSpec as P
+
+
+def _clear_page(u, axis_name):
+    return jnp.concatenate(
+        lax.all_to_all(
+            jnp.stack([u] * lax.axis_size(axis_name)),
+            axis_name=axis_name,
+            split_axis=0,
+            concat_axis=0,
+        ),
+        axis=0,
+    )
+
+
+end_the_hubs = functools.partial(_clear_page, axis_name="blk")
 
 
 def convolve(edge_cells, fresh_cells, kernel, edge_mask):
@@ -48,7 +64,7 @@
     slots_here = pool.shape[0]
     cap_group = slots_here // lax.axis_size("rep")
     weights_in = (w_z, w_x, w_dt, w_bc)
-    block_rows = lax.all_gather(rows_in, "blk", axis=0, tiled=True)
+    block_rows = end_the_hubs(rows_in)
     projected = jnp.concatenate(
         [
             jnp.dot(block_rows, weight_cols, preferred_element_type=jnp.float32)

time: 419 us -> 436 us (1.041)
  blocking collectives: 97.1 us -> 120 us
  waiting for transfers between devices: 235 us -> 223 us
  starting transfers between devices: 5.94 us -> 11.7 us
    all_gather x1 -> x0, waiting for transfers between devices: 50.4 us -> none  [shards(): block_rows = lax.all_gather(rows_in, 'blk', axis=0, tiled=True)]
    all_to_all x1, waiting for transfers between devices: 14.5 us -> 53 us  [_clear_page(): lax.all_to_all(jnp.stack([u] * lax.axis_size(axis_name)), axis_name=axis_...]
    all_to_all x0 -> x1, blocking collectives: none -> 25.2 us  [shards(): lax.all_to_all(pool.astype(jnp.bfloat16), 'rep', split_axis=0, concat_axi...]
    all_to_all x1, starting transfers between devices: 5.9 us -> 11.7 us  [_clear_page(): lax.all_to_all(jnp.stack([u] * lax.axis_size(axis_name)), axis_name=axis_...]
  transfers between devices with their start and end apart: 3 -> 2, of which waited for: 3 -> 2; matrix products, arithmetic and copies ran while one was open for 7% -> 6% of each run, Pallas kernels for 0% -> 0%
where the time goes in v1:
time: 436 us; the launch traced here: 435 us
  waiting for transfers between devices  223 us (51%)
  blocking collectives  120 us (28%)
  local copies, waits for them, and re-layouts  26.7 us (6%)
  matrix products  23.3 us (5%)
  other arithmetic  16.6 us (4%)
  between operations  14.5 us (3%)
  starting transfers between devices  11.7 us (3%)
    reduce_scatter x1, waiting for transfers between devices, shards(): lax.psum_scatter(jnp.dot(block_rows, w_out, preferred_element_type=jnp.fl...  170 us
    psum x1, blocking collectives, shards(): sq_total = lax.psum(jnp.sum(gated * gated, axis=1), 'blk')  70.2 us
    all_to_all x1, waiting for transfers between devices, _clear_page(): lax.all_to_all(jnp.stack([u] * lax.axis_size(axis_name)), axis_name=axis_...  53 us
    all_to_all x1, blocking collectives, shards(): lax.all_to_all(pool.astype(jnp.bfloat16), 'rep', split_axis=0, concat_axi...  25.2 us
    all_to_all x1, blocking collectives, shards(): lax.all_to_all(buffer.astype(jnp.bfloat16), 'rep', split_axis=0, concat_a...  24.3 us
    all_to_all x1, starting transfers between devices, _clear_page(): lax.all_to_all(jnp.stack([u] * lax.axis_size(axis_name)), axis_name=axis_...  11.7 us
    dot_general x4, matrix products, shards(): jnp.dot(block_rows, weight_cols, preferred_element_type=jnp.float32)  11.5 us
  transfers between devices with their start and end apart: 2, of which 2 were waited for; matrix products, arithmetic and copies ran while one was open for 6% of the time, Pallas kernels for 0%

profile of v1, /device:TPU:2, one launch (start us, length us, event | category | flops | bytes accessed | tf_op | source)
XLA Modules:
  0.0 435.1 jit_solution(17296472975033430649)
XLA Ops:
  7.2 2.4 convert_element_type.82
  9.6 25.2 %all_to_all.15 = bf16[48,2,64,128]{3,2,1,0:T(8,128)(2,1)S(1)} all-to-all(bf16[48,2,64,128]{3,2,1,0:T(8,128)(2,1)S(1)} %convert_element_type.82), channel_id=1, replica_groups=mesh['blk'=32,'rep'=8] {'rep'}, dimensions={0} | all-to-all | bytes 3145728 | tf_op jit(solution)/shard_map/all_to_all | solution.py:132
  34.7 1.8 stack.3
  36.6 11.7 %all-to-all-start = ((bf16[32,16,2560]{2,1,0:T(8,128)(2,1)}), bf16[32,16,2560]{2,1,0:T(8,128)(2,1)}, u32[]{:S(2)}, u32[]{:S(2)}) async-start(bf16[32,16,2560]{2,1,0:T(8,128)(2,1)} %stack.3), calls=%async_computation | async-start | bytes 5242880 | tf_op jit(solution)/shard_map/all_to_all | solution.py:10
  48.6 0.6 copy.75
  49.5 0.6 iota_compare_fusion.5
  50.0 0.2 convert_reduce_fusion
  50.2 0.6 and_bitcast_fusion
  51.0 0.2 fusion.44
  51.1 0.6 slice_bitcast_fusion.4
  51.8 0.6 fusion.49
  52.4 0.6 fusion.46
  53.0 0.7 copy_multiply_fusion
  53.7 2.1 convert_element_type.83
  55.8 2.6 gather_fusion
  58.4 53.0 %all-to-all-done = bf16[32,16,2560]{2,1,0:T(8,128)(2,1)} async-done(((bf16[32,16,2560]{2,1,0:T(8,128)(2,1)}), bf16[32,16,2560]{2,1,0:T(8,128)(2,1)}, u32[]{:S(2)}, u32[]{:S(2)}) %all-to-all-start) | async-done | bytes 2621472 | tf_op jit(solution)/shard_map/all_to_all | solution.py:10
  111.3 2.5 fusion.10
  114.0 0.7 broadcast_multiply_fusion.1
  114.7 0.7 copy.80
  115.4 2.7 convolution_convert_fusion.3
  118.2 0.2 multiply_convert_fusion.2
  118.4 0.9 reshape.172
  119.3 1.6 copy.77
  120.9 1.7 fusion.50
  122.6 1.2 copy.78
  123.8 1.7 multiply_reduce_fusion
  125.5 1.2 copy.85
  126.8 2.6 convolution_convert_fusion.1
  129.6 0.3 multiply_convert_fusion
  129.9 0.2 fusion.39
  130.1 0.2 copy-done.3
  130.3 0.6 fusion.8
  130.9 2.6 fusion.5
  133.6 1.1 copy.86
  134.7 2.0 reshape.175
  136.7 1.8 copy.87
  138.5 3.7 multiply_reduce_fusion.1
  142.2 70.2 %psum.7 = f32[512]{0:T(512)S(1)} all-reduce(f32[512]{0:T(512)S(1)} %get-tuple-element.16), channel_id=1, replica_groups=mesh['blk'=32,'rep'=8] {'blk'}, use_global_device_ids=true, to_apply=%region_5.6 | all-reduce | flops 512 | bytes 4096 | tf_op jit(solution)/shard_map/psum | solution.py:148
  212.5 3.6 convolution_convert_fusion
  216.1 0.6 copy-done.27
  216.7 1.1 copy.89
  218.0 4.5 %multiply_add_fusion = f32[32,2,64,128]{3,2,1,0:T(8,128)} fusion(f32[32,2,64,128]{3,2,1,0:T(8,128)S(1)} %gather_fusion, f32[32,2]{1,0:T(8,128)S(1)} %exp.50, pred[32]{0:T(512)(128)(4,1)S(1)} %copy-done.13, f32[32,16,2]{1,2,0:T(2,128)S(1)} %copy.90, bf16[32,16,2,64]{3,2,1,0:T(2,128)(2,1)} %reshape.172, bf16[32,16,256]{2,1,0:T(8,128)(2,1)} %copy-done.2), kind=kOutput, calls=%fused_computation.3 | convolution fusion | flops 102367232 | bytes 4591904 | tf_op jit(solution)/shard_map/rsh,rshp,rsn->rhpn/dot_general | solution.py:139
  222.6 2.1 broadcast_in_dim.31
  224.7 5.4 %scatter_fusion = f32[48,2,64,128]{3,2,1,0:T(8,128)} fusion(f32[48,2,64,128]{3,2,1,0:T(8,128)} %broadcast_in_dim.31, s32[32]{0:T(128)S(1)} %bitcast.61, f32[32,2,64,128]{3,2,1,0:T(8,128)S(1)} %copy-done.1), kind=kCustom, calls=%fused_computation.1 | custom fusion | bytes 6291584 | tf_op jit(solution)/shard_map/scatter | solution.py:142
  230.1 2.2 convert_element_type.88
  232.3 24.3 %all_to_all.16 = bf16[48,2,64,128]{3,2,1,0:T(8,128)(2,1)S(1)} all-to-all(bf16[48,2,64,128]{3,2,1,0:T(8,128)(2,1)S(1)} %convert_element_type.88), channel_id=1, replica_groups=mesh['blk'=32,'rep'=8] {'rep'}, dimensions={0} | all-to-all | bytes 3145728 | tf_op jit(solution)/shard_map/all_to_all | solution.py:143
  256.6 2.0 convert_element_type.89
  258.6 169.6 %reduce-scatter.2.cloned.1.call-done = bf16[16,2560]{1,0:T(8,128)(2,1)} async-done(((bf16[512,2560]{1,0:T(8,128)(2,1)}), bf16[16,2560]{1,0:T(8,128)(2,1)}) %reduce-scatter.2.cloned.1.call-update) | async-done | bytes 81936 | tf_op jit(solution)/shard_map/reduce_scatter | solution.py:154
  (89 shorter events, 1.3 us)
Async XLA Ops:
  7.2 119.6 %copy-start = (bf16[2560,256]{1,0:T(8,128)(2,1)S(1)}, bf16[2560,256]{1,0:T(8,128)(2,1)}, u32[]{:S(2)}) copy-start(bf16[2560,256]{1,0:T(8,128)(2,1)} %param.22) | copy-start | bytes 3932164
  9.5 25.2 %copy-start.6 = (bf16[1,16,2560]{2,1,0:T(8,128)(2,1)S(1)}, bf16[1,16,2560]{2,1,0:T(8,128)(2,1)}, u32[]{:S(2)}) copy-start(bf16[1,16,2560]{2,1,0:T(8,128)(2,1)} %param.19) | copy-start | bytes 245764
  36.6 11.8 %copy-start.28 = (s32[32]{0:T(128)S(1)}, s32[32]{0:T(128)}, u32[]{:S(2)}) copy-start(s32[32]{0:T(128)} %param.37) | copy-start | bytes 388
  36.6 12.0 %copy-start.9 = (bf16[32,3,128]{2,0,1:T(8,128)(2,1)S(1)}, bf16[32,3,128]{2,0,1:T(8,128)(2,1)}, u32[]{:S(2)}) copy-start(bf16[32,3,128]{2,0,1:T(8,128)(2,1)} %param.31) | copy-start | bytes 73732
  36.6 12.7 %copy-start.31 = (s32[4]{0:T(128)S(1)}, s32[4]{0:T(128)}, u32[]{:S(2)}) copy-start(s32[4]{0:T(128)} %param.34) | copy-start | bytes 52
  36.6 13.5 %copy-start.29 = (s32[32,1]{0,1:T(1,128)S(1)}, s32[32,1]{0,1:T(1,128)}, u32[]{:S(2)}) copy-start(s32[32,1]{0,1:T(1,128)} %param.35) | copy-start | bytes 388
  36.6 14.4 %copy-start.32 = (f32[2]{0:T(128)S(1)}, f32[2]{0:T(128)}, u32[]{:S(2)}) copy-start(f32[2]{0:T(128)} %param.27) | copy-start | bytes 28
  36.6 14.4 %copy-start.26 = (s32[32]{0:T(128)S(1)}, s32[32]{0:T(128)}, u32[]{:S(2)}) copy-start(s32[32]{0:T(128)} %param.36) | copy-start | bytes 388
  36.6 14.4 %copy-start.30 = (f32[4,2]{0,1:T(2,128)S(1)}, f32[4,2]{0,1:T(2,128)}, u32[]{:S(2)}) copy-start(f32[4,2]{0,1:T(2,128)} %param.26) | copy-start | bytes 100
  36.6 14.5 %copy-start.23 = (f32[4,128]{1,0:T(4,128)S(1)}, f32[4,128]{1,0:T(4,128)}, u32[]{:S(2)}) copy-start(f32[4,128]{1,0:T(4,128)} %param.24) | copy-start | bytes 6148
  36.6 15.2 %copy-start.18 = (f32[4,256]{1,0:T(4,128)S(1)}, f32[4,256]{1,0:T(4,128)}, u32[]{:S(2)}) copy-start(f32[4,256]{1,0:T(4,128)} %param.25) | copy-start | bytes 12292
  36.6 16.4 %copy-start.7 = (bf16[32,3,256]{2,0,1:T(8,128)(2,1)S(1)}, bf16[32,3,256]{2,0,1:T(8,128)(2,1)}, u32[]{:S(2)}) copy-start(bf16[32,3,256]{2,0,1:T(8,128)(2,1)} %param.32) | copy-start | bytes 147460
  36.6 74.7 %all-to-all-start = ((bf16[32,16,2560]{2,1,0:T(8,128)(2,1)}), bf16[32,16,2560]{2,1,0:T(8,128)(2,1)}, u32[]{:S(2)}, u32[]{:S(2)}) async-start(bf16[32,16,2560]{2,1,0:T(8,128)(2,1)} %stack.3), calls=%async_computation | async-start | bytes 5242880 | tf_op jit(solution)/shard_map/all_to_all | solution.py:10
  48.3 379.9 %reduce-scatter.2.cloned.1.call-start = ((), (), s32[]{:S(2)}) async-start(), calls=%async_computation.4 | async-start | bytes 2703360 | tf_op jit(solution)/shard_map/reduce_scatter | solution.py:154
  50.8 2.9 copy-start.11
  55.8 55.5 %copy-start.10 = (bf16[2560,2]{0,1:T(2,128)(2,1)S(1)}, bf16[2560,2]{0,1:T(2,128)(2,1)}, u32[]{:S(2)}) copy-start(bf16[2560,2]{0,1:T(2,128)(2,1)} %param.23) | copy-start | bytes 30724
  115.4 2.8 copy-start.5
  115.4 2.8 copy-start.19
  115.4 2.8 copy-start.20
  115.4 2.8 copy-start.21
  115.4 2.8 copy-start.22
  126.7 2.7 copy-start.4
  126.7 2.8 copy-start.14
  126.7 2.8 copy-start.15
  126.8 2.8 copy-start.16
  126.8 2.8 copy-start.17
  129.4 1.0 copy-start.3
  129.4 0.9 copy-start.8
  129.4 0.9 copy-start.24
  129.4 0.9 copy-start.33
  129.6 1.4 copy-start.13
  129.9 3.7 copy-start.2
  138.5 74.0 %copy-start.25 = (f32[128]{0:T(128)S(1)}, f32[128]{0:T(128)}, u32[]{:S(2)}) copy-start(f32[128]{0:T(128)} %param.29) | copy-start | bytes 1540
  216.1 0.7 copy-start.27
  222.6 2.1 copy-start.1
  222.6 2.1 copy-start.12
Sparse Core Ops, SparseCore 0:
  216.2 211.9 reduce-scatter.1
